TPU v7x, 512 devices: a whole 4x8x8 slice. The times are simulated.
512 devices in a mesh: dp: 8 (over z_lo, x), region: 64 (over y, z_hi, core).
Axes of the slice: x: 4, y: 8, z: 8 (z_hi: 4, z_lo: 2; z = z_hi * 2 + z_lo), core: 2. Of those that a mesh axis runs over, the one named last changes fastest.
Arguments:
- queries: bfloat16 [8, 8192, 1280], P('dp', 'region'), may hold values from -5 to 5
- keys: bfloat16 [8, 8192, 1280], P('dp', 'region'), may hold values from -5 to 5
- values: bfloat16 [8, 8192, 1280], P('dp', 'region'), may hold values from -6 to 6
- attn_out: bfloat16 [8, 8192, 1280], P('dp', 'region'), may hold values from -0.125 to 0.125
- d_out: bfloat16 [8, 8192, 2560], P('dp', 'region'), may hold values from -6 to 6
- w_out: bfloat16 [1280, 2560], P('dp'), may hold values from -0.15625 to 0.15625
- adjacency: int32 [64, 4, 12], P('region'), may hold values from 0 to 1, as said below
- counts: int32 [64], P('region'), may hold values from 1 to 4, as said below
Outputs:
- d_queries: bfloat16 [8, 8192, 1280], P('dp', 'region')
- d_keys: bfloat16 [8, 8192, 1280], P('dp', 'region')
- d_values: bfloat16 [8, 8192, 1280], P('dp', 'region')
- d_weight: bfloat16 [1280, 2560], P('dp')
Inputs may be any that keep to these rules, and one draw needn't show every extreme that they name: Region r has 4 token blocks, of which the first counts[r] are live; in some region all 4 are live. adjacency[r, a, j] = 1 lets query block a of region r see key block j % 4 of region (r + j // 4 - 1) mod 64; entry j = 4 + a is 1.
All inputs are finite; a program needn't handle non-finite values.
Results may differ from a plain program's by a relative error of at most 0.007.
Values may be sent and summed in bfloat16 or wider, within the bound.
No kernel may reach another device: no remote copies, remote signals or barrier semaphores. Data moves between devices by JAX's collectives and lax.ppermute only.
A program may use at most 64 MiB of HBM per device.

v0:
```python
import math
import jax
import jax.numpy as jnp
from jax import lax
from jax.sharding import PartitionSpec as P

HEADS = 8
HD = 160
BLK = 4


def from_behind(value, axis, by):
    length = lax.axis_size(axis)
    return lax.ppermute(value, axis, [(i, (i + by) % length) for i in range(length)])


def expand(blocks, block_rows):
    return jnp.repeat(jnp.repeat(blocks, block_rows, axis=0), block_rows, axis=1)


def score_block(query_rows, key_rows):
    scores = jnp.einsum("qhc,khc->hqk", query_rows, key_rows, preferred_element_type=jnp.float32)
    return scores * (1.0 / math.sqrt(HD))


def row_stats(scores, allowed):
    maxima = jnp.max(jnp.where(allowed[None], scores, -1e30), axis=2)
    totals = jnp.sum(jnp.exp(jnp.where(allowed[None], scores - maxima[:, :, None], -1e30)), axis=2)
    return (maxima, totals)


def backward_block(scores, allowed, lse, delta, query_rows, key_rows, value_rows, grad_rows):
    probs = jnp.exp(jnp.where(allowed[None], scores - lse[:, :, None], -1e30))
    probs_b = probs.astype(jnp.bfloat16)
    dvalue = jnp.einsum("hqk,qhc->khc", probs_b, grad_rows, preferred_element_type=jnp.float32)
    dprobs = jnp.einsum("qhc,khc->hqk", grad_rows, value_rows, preferred_element_type=jnp.float32)
    dscores = (probs * (dprobs - delta[:, :, None]) * (1.0 / math.sqrt(HD))).astype(jnp.bfloat16)
    dquery = jnp.einsum("hqk,khc->qhc", dscores, key_rows, preferred_element_type=jnp.float32)
    dkey = jnp.einsum("hqk,qhc->khc", dscores, query_rows, preferred_element_type=jnp.float32)
    return (dquery, dkey, dvalue)


def local(queries, keys, values, attn_out, d_out, w_out, adjacency, counts):
    tok_rows = queries.shape[1]
    block_rows = tok_rows // BLK
    width = queries.shape[2]
    live_blocks = jnp.arange(BLK) < counts[0]
    live_rows = jnp.repeat(live_blocks, block_rows)
    grads = d_out * live_rows[None, :, None].astype(jnp.bfloat16)
    gathered = lax.all_gather(grads, "dp", axis=1, tiled=True)
    out_cols = lax.all_to_all(attn_out, "dp", split_axis=2, concat_axis=1, tiled=True)
    attn_part = jnp.einsum("td,hd->th", gathered[0], w_out, preferred_element_type=jnp.float32)
    d_attn = lax.all_to_all(
        attn_part.astype(jnp.bfloat16)[None], "dp", split_axis=1, concat_axis=2, tiled=True
    )
    weight_part = jnp.einsum(
        "th,td->hd", out_cols[0], gathered[0], preferred_element_type=jnp.float32
    )
    d_weight = lax.psum(weight_part, "region").astype(jnp.bfloat16)
    query_rows = queries[0].reshape(tok_rows, HEADS, HD)
    out_rows = attn_out[0].reshape(tok_rows, HEADS, HD)
    grad_attn = d_attn[0].reshape(tok_rows, HEADS, HD)
    delta = jnp.einsum("qhc,qhc->hq", grad_attn, out_rows, preferred_element_type=jnp.float32)
    adjacent = adjacency[0] == 1
    own_block = jnp.arange(3 * BLK)[None, :] == BLK + jnp.arange(BLK)[:, None]
    key_live = live_rows.astype(jnp.bfloat16)
    fetched = {}
    for offset in (1, -1):
        fetched[offset] = from_behind((keys[0], values[0], key_live), "region", offset)
    key_window = jnp.concatenate([fetched[1][0], keys[0], fetched[-1][0]], 0).reshape(
        3 * tok_rows, HEADS, HD
    )
    value_window = jnp.concatenate([fetched[1][1], values[0], fetched[-1][1]], 0).reshape(
        3 * tok_rows, HEADS, HD
    )
    live_window = jnp.concatenate([fetched[1][2], key_live, fetched[-1][2]], 0)
    live_window = live_window.reshape(3 * BLK, block_rows)[:, 0] > 0.5
    allowed = expand(adjacent & live_window[None] | own_block, block_rows)
    scores = score_block(query_rows, key_window)
    maxima, totals = row_stats(scores, allowed)
    lse = maxima + jnp.log(totals)
    dquery, dkey_win, dvalue_win = backward_block(
        scores, allowed, lse, delta, query_rows, key_window, value_window, grad_attn
    )
    dkey = dkey_win[tok_rows : 2 * tok_rows]
    dvalue = dvalue_win[tok_rows : 2 * tok_rows]
    for offset, first in ((-1, 0), (1, 2)):
        lower = first * tok_rows
        returned = (
            from_behind(
                dkey_win[lower : lower + tok_rows].astype(jnp.bfloat16), "region", offset
            ).astype(jnp.float32),
            from_behind(
                dvalue_win[lower : lower + tok_rows].astype(jnp.bfloat16), "region", offset
            ).astype(jnp.float32),
        )
        dkey = dkey + returned[0]
        dvalue = dvalue + returned[1]
    out_shape = (1, tok_rows, width)
    return (
        dquery.astype(jnp.bfloat16).reshape(out_shape),
        dkey.astype(jnp.bfloat16).reshape(out_shape),
        dvalue.astype(jnp.bfloat16).reshape(out_shape),
        d_weight,
    )


def solution(mesh):
    return jax.shard_map(
        local,
        mesh=mesh,
        in_specs=(
            P("dp", "region", None),
            P("dp", "region", None),
            P("dp", "region", None),
            P("dp", "region", None),
            P("dp", "region", None),
            P("dp", None),
            P("region", None, None),
            P("region"),
        ),
        out_specs=(
            P("dp", "region", None),
            P("dp", "region", None),
            P("dp", "region", None),
            P("dp", None),
        ),
        check_vma=False,
    )
```

profile of v0, /device:TPU:2, one launch (start us, length us, event | category | flops | bytes accessed | tf_op | source)
XLA Modules:
  0.0 473.0 jit_solution(7799400725067004841)
XLA Ops:
  8.2 2.0 broadcast_multiply_fusion
  10.3 13.3 %collective-permute-start.3 = (bf16[128]{0:T(256)(128)(2,1)S(1)}, bf16[128]{0:T(256)(128)(2,1)S(1)}, u32[]{:S(2)}, u32[]{:S(2)}) collective-permute-start(bf16[128]{0:T(256)(128)(2,1)S(1)} %convert_element_type.56), channel_id=1, source_target_pairs={{0,63},{1,0},{2,1},{3,2},{4,3},{5,4},{6,5},{7,6},{8,7},{9,8},{10,9... | collective-permute-start | bytes 776 | tf_op jit(solution)/shard_map/ppermute | solution.py:14
  23.6 2.6 collective-permute-start.1
  26.1 1.9 collective-permute-start
  28.1 7.9 %collective-permute-start.5 = (bf16[128,1280]{1,0:T(8,128)(2,1)S(1)}, bf16[128,1280]{1,0:T(8,128)(2,1)}, u32[]{:S(2)}, u32[]{:S(2)}) collective-permute-start(bf16[128,1280]{1,0:T(8,128)(2,1)S(1)} %bitcast.121), channel_id=1, source_target_pairs={{0,63},{1,0},{2,1},{3,2},{4,3},{5,4},{6,5},{7,6},{8,7},{9,8},{10,9... | collective-permute-start | bytes 983048 | tf_op jit(solution)/shard_map/ppermute | solution.py:14
  36.0 1.9 collective-permute-start.4
  39.0 7.5 %reduce.5 = bf16[1280,128]{1,0:T(8,128)(2,1)S(1)} reduce(bf16[1280,1,128]{2,1,0:T(2,128)(2,1)S(1)} %bitcast.106, bf16[]{:T(256)} %broadcast.40), dimensions={1}, to_apply=%bitcast.90.reduce_sub_computation | reduce | bytes 655362
  47.3 5.9 %all-to-all-start.1 = ((bf16[8,2,10240]{2,1,0:T(2,128)(2,1)}), bf16[8,2,10240]{2,1,0:T(2,128)(2,1)S(1)}, u32[]{:S(2)}, u32[]{:S(2)}) async-start(bf16[8,2,10240]{2,1,0:T(2,128)(2,1)} %reshape.81), calls=%async_computation.1 | async-start | bytes 655360 | tf_op jit(solution)/shard_map/all_to_all | solution.py:51
  53.4 2.1 collective-permute-start.2
  57.7 4.8 %collective-permute-done.2 = bf16[128]{0:T(256)(128)(2,1)S(1)} collective-permute-done((bf16[128]{0:T(256)(128)(2,1)S(1)}, bf16[128]{0:T(256)(128)(2,1)S(1)}, u32[]{:S(2)}, u32[]{:S(2)}) %collective-permute-start.2) | collective-permute-done | bytes 288 | tf_op jit(solution)/shard_map/ppermute | solution.py:14
  63.3 1.3 copy.67
  64.7 2.0 copy.77
  66.7 1.9 copy.75
  69.3 1.2 copy-done.2
  71.8 20.1 %all-gather.2.cloned.1.call-done = bf16[1,1024,2560]{2,1,0:T(8,128)(2,1)} async-done(((bf16[1,128,2560]{2,1,0:T(8,128)(2,1)}), bf16[1,1024,2560]{2,1,0:T(8,128)(2,1)}) %all-gather.2.cloned.1.call-update) | async-done | bytes 5242896 | tf_op jit(solution)/shard_map/all_gather | solution.py:50
  92.0 3.6 fusion.4
  96.0 2.6 fusion.17
  98.6 2.4 copy.72
  100.9 4.9 %reduce.4 = bf16[1024,160]{1,0:T(8,128)(2,1)} reduce(bf16[1024,1,160]{2,1,0:T(2,128)(2,1)S(1)} %bitcast.104, bf16[]{:T(256)} %broadcast.40), dimensions={1}, to_apply=%bitcast.88.reduce_sub_computation | reduce | bytes 655362
  105.8 2.6 reshape.79
  108.4 10.2 %all-to-all-start = ((bf16[8,2,10240]{2,1,0:T(2,128)(2,1)}), bf16[8,2,10240]{2,1,0:T(2,128)(2,1)S(1)}, u32[]{:S(2)}, u32[]{:S(2)}) async-start(bf16[8,2,10240]{2,1,0:T(2,128)(2,1)} %reshape.79), calls=%async_computation | async-start | bytes 655360 | tf_op jit(solution)/shard_map/all_to_all | solution.py:53
  118.5 307.2 %all-reduce.1 = bf16[160,2560]{1,0:T(8,128)(2,1)} all-reduce(f32[160,2560]{1,0:T(8,128)S(1)} %fusion.4), channel_id=1, replica_groups=mesh['dp'=8,'region'=64] {'region'}, use_global_device_ids=true, to_apply=%region_2.3 | all-reduce | flops 409600 | bytes 2457600 | tf_op jit(solution)/shard_map/psum | solution.py:59
  425.7 2.1 reshape.80
  427.8 1.4 copy.104
  430.5 1.8 fusion.46
  433.2 2.1 collective-permute-start.8
  435.3 2.4 collective-permute-start.9
  440.2 7.6 %collective-permute-start.6 = (bf16[128,8,160]{0,2,1:T(8,128)(2,1)}, bf16[128,8,160]{0,2,1:T(8,128)(2,1)}, u32[]{:S(2)}, u32[]{:S(2)}) collective-permute-start(bf16[128,8,160]{0,2,1:T(8,128)(2,1)} %get-tuple-element.22), channel_id=1, source_target_pairs={{0,63},{1,0},{2,1},{3,2},{4,3},{5,4},{6,5},{7,6},{8,7},{9,8},{10,9... | collective-permute-start | bytes 983048 | tf_op jit(solution)/shard_map/ppermute | solution.py:14
  447.8 1.9 collective-permute-start.7
  451.8 1.4 fusion.30
  454.1 9.9 %collective-permute-done.7 = bf16[128,8,160]{0,2,1:T(8,128)(2,1)} collective-permute-done((bf16[128,8,160]{0,2,1:T(8,128)(2,1)S(1)}, bf16[128,8,160]{0,2,1:T(8,128)(2,1)}, u32[]{:S(2)}, u32[]{:S(2)}) %collective-permute-start.7) | collective-permute-done | bytes 327712 | tf_op jit(solution)/shard_map/ppermute | solution.py:14
  464.0 1.2 fusion.32
  (94 shorter events, 16.2 us)
Async XLA Ops:
  7.2 88.4 %copy-start = (bf16[160,2560]{1,0:T(8,128)(2,1)S(1)}, bf16[160,2560]{1,0:T(8,128)(2,1)}, u32[]{:S(2)}) copy-start(bf16[160,2560]{1,0:T(8,128)(2,1)} %param.13) | copy-start | bytes 2457604
  7.2 16.4 %copy-start.10 = (bf16[1,128,1280]{2,1,0:T(8,128)(2,1)S(1)}, bf16[1,128,1280]{2,1,0:T(8,128)(2,1)}, u32[]{:S(2)}) copy-start(bf16[1,128,1280]{2,1,0:T(8,128)(2,1)} %param.9) | copy-start | bytes 983044
  7.2 20.9 %copy-start.11 = (bf16[1,128,1280]{2,1,0:T(8,128)(2,1)S(1)}, bf16[1,128,1280]{2,1,0:T(8,128)(2,1)}, u32[]{:S(2)}) copy-start(bf16[1,128,1280]{2,1,0:T(8,128)(2,1)} %param.10) | copy-start | bytes 983044
  7.2 30.7 %copy-start.6 = (bf16[1,128,1280]{2,1,0:T(8,128)(2,1)S(1)}, bf16[1,128,1280]{2,1,0:T(8,128)(2,1)}, u32[]{:S(2)}) copy-start(bf16[1,128,1280]{2,1,0:T(8,128)(2,1)} %param.11) | copy-start | bytes 983044
  7.2 84.7 %all-gather.2.cloned.1.call-start = ((), (), s32[]{:S(2)}) async-start(), calls=%async_computation.2 | async-start | bytes 5898240 | tf_op jit(solution)/shard_map/all_gather | solution.py:50
  10.3 43.2 %collective-permute-start.3 = (bf16[128]{0:T(256)(128)(2,1)S(1)}, bf16[128]{0:T(256)(128)(2,1)S(1)}, u32[]{:S(2)}, u32[]{:S(2)}) collective-permute-start(bf16[128]{0:T(256)(128)(2,1)S(1)} %convert_element_type.56), channel_id=1, source_target_pairs={{0,63},{1,0},{2,1},{3,2},{4,3},{5,4},{6,5},{7,6},{8,7},{9,8},{10,9... | collective-permute-start | bytes 776 | tf_op jit(solution)/shard_map/ppermute | solution.py:14
  23.6 39.5 %collective-permute-start.1 = (bf16[128,1280]{1,0:T(8,128)(2,1)S(1)}, bf16[128,1280]{1,0:T(8,128)(2,1)S(1)}, u32[]{:S(2)}, u32[]{:S(2)}) collective-permute-start(bf16[128,1280]{1,0:T(8,128)(2,1)S(1)} %bitcast.119), channel_id=1, source_target_pairs={{0,63},{1,0},{2,1},{3,2},{4,3},{5,4},{6,5},{7,6},{8,7},{9,8},{10,9... | collective-permute-start | bytes 983048 | tf_op jit(solution)/shard_map/ppermute | solution.py:14
  26.1 37.2 %collective-permute-start = (bf16[128,1280]{1,0:T(8,128)(2,1)S(1)}, bf16[128,1280]{1,0:T(8,128)(2,1)}, u32[]{:S(2)}, u32[]{:S(2)}) collective-permute-start(bf16[128,1280]{1,0:T(8,128)(2,1)S(1)} %bitcast.120), channel_id=1, source_target_pairs={{0,1},{1,2},{2,3},{3,4},{4,5},{5,6},{6,7},{7,8},{8,9},{9,10},{10,1... | collective-permute-start | bytes 983048 | tf_op jit(solution)/shard_map/ppermute | solution.py:14
  28.1 36.6 %collective-permute-start.5 = (bf16[128,1280]{1,0:T(8,128)(2,1)S(1)}, bf16[128,1280]{1,0:T(8,128)(2,1)}, u32[]{:S(2)}, u32[]{:S(2)}) collective-permute-start(bf16[128,1280]{1,0:T(8,128)(2,1)S(1)} %bitcast.121), channel_id=1, source_target_pairs={{0,63},{1,0},{2,1},{3,2},{4,3},{5,4},{6,5},{7,6},{8,7},{9,8},{10,9... | collective-permute-start | bytes 983048 | tf_op jit(solution)/shard_map/ppermute | solution.py:14
  36.0 30.7 %collective-permute-start.4 = (bf16[128,1280]{1,0:T(8,128)(2,1)S(1)}, bf16[128,1280]{1,0:T(8,128)(2,1)}, u32[]{:S(2)}, u32[]{:S(2)}) collective-permute-start(bf16[128,1280]{1,0:T(8,128)(2,1)S(1)} %bitcast.122), channel_id=1, source_target_pairs={{0,1},{1,2},{2,3},{3,4},{4,5},{5,6},{6,7},{7,8},{8,9},{9,10},{10,1... | collective-permute-start | bytes 983048 | tf_op jit(solution)/shard_map/ppermute | solution.py:14
  46.5 10.9 %copy-start.9 = (bf16[1,128,1280]{2,1,0:T(8,128)(2,1)S(1)}, bf16[1,128,1280]{2,1,0:T(8,128)(2,1)}, u32[]{:S(2)}) copy-start(bf16[1,128,1280]{2,1,0:T(8,128)(2,1)} %param.8) | copy-start | bytes 983044
  47.3 15.4 %copy-start.22 = (s32[1,4,12]{2,1,0:T(4,128)S(1)}, s32[1,4,12]{2,1,0:T(4,128)}, u32[]{:S(2)}) copy-start(s32[1,4,12]{2,1,0:T(4,128)} %param.14) | copy-start | bytes 580
  47.3 24.0 %all-to-all-start.1 = ((bf16[8,2,10240]{2,1,0:T(2,128)(2,1)}), bf16[8,2,10240]{2,1,0:T(2,128)(2,1)S(1)}, u32[]{:S(2)}, u32[]{:S(2)}) async-start(bf16[8,2,10240]{2,1,0:T(2,128)(2,1)} %reshape.81), calls=%async_computation.1 | async-start | bytes 655360 | tf_op jit(solution)/shard_map/all_to_all | solution.py:51
  53.4 15.1 %copy-start.12 = (bf16[1,128,1280]{1,2,0:T(8,128)(2,1)}, bf16[1,128,1280]{1,2,0:T(8,128)(2,1)S(1)}, u32[]{:S(2)}) copy-start(bf16[1,128,1280]{1,2,0:T(8,128)(2,1)S(1)} %copy.68) | copy-start | bytes 983044
  53.4 9.1 %collective-permute-start.2 = (bf16[128]{0:T(256)(128)(2,1)S(1)}, bf16[128]{0:T(256)(128)(2,1)S(1)}, u32[]{:S(2)}, u32[]{:S(2)}) collective-permute-start(bf16[128]{0:T(256)(128)(2,1)S(1)} %convert_element_type.56), channel_id=1, source_target_pairs={{0,1},{1,2},{2,3},{3,4},{4,5},{5,6},{6,7},{7,8},{8,9},{9,10},{10,1... | collective-permute-start | bytes 776 | tf_op jit(solution)/shard_map/ppermute | solution.py:14
  57.6 11.6 %copy-start.7 = (bf16[1,128,1280]{1,2,0:T(8,128)(2,1)}, bf16[1,128,1280]{1,2,0:T(8,128)(2,1)S(1)}, u32[]{:S(2)}) copy-start(bf16[1,128,1280]{1,2,0:T(8,128)(2,1)S(1)} %copy.71) | copy-start | bytes 983044
  63.3 5.9 %copy-start.15 = (bf16[128,1280]{0,1:T(8,128)(2,1)}, bf16[128,1280]{0,1:T(8,128)(2,1)S(1)}, u32[]{:S(2)}) copy-start(bf16[128,1280]{0,1:T(8,128)(2,1)S(1)} %copy.69) | copy-start | bytes 983044
  64.6 4.6 copy-start.17
  92.0 4.0 copy-start.1
  108.4 317.4 %all-to-all-start = ((bf16[8,2,10240]{2,1,0:T(2,128)(2,1)}), bf16[8,2,10240]{2,1,0:T(2,128)(2,1)S(1)}, u32[]{:S(2)}, u32[]{:S(2)}) async-start(bf16[8,2,10240]{2,1,0:T(2,128)(2,1)} %reshape.79), calls=%async_computation | async-start | bytes 655360 | tf_op jit(solution)/shard_map/all_to_all | solution.py:53
  430.4 7.3 %copy-start.4 = (bf16[1,128,1280]{1,2,0:T(8,128)(2,1)S(1)}, bf16[1,128,1280]{1,2,0:T(8,128)(2,1)}, u32[]{:S(2)}) copy-start(bf16[1,128,1280]{1,2,0:T(8,128)(2,1)} %copy.102) | copy-start | bytes 983044
  430.4 7.3 %copy-start.5 = (bf16[8,128,160]{1,2,0:T(8,128)(2,1)S(1)}, bf16[8,128,160]{1,2,0:T(8,128)(2,1)}, u32[]{:S(2)}) copy-start(bf16[8,128,160]{1,2,0:T(8,128)(2,1)} %copy.101) | copy-start | bytes 983044
  432.2 5.6 %copy-start.14 = (bf16[1,128,1280]{1,2,0:T(8,128)(2,1)S(1)}, bf16[1,128,1280]{1,2,0:T(8,128)(2,1)}, u32[]{:S(2)}) copy-start(bf16[1,128,1280]{1,2,0:T(8,128)(2,1)} %copy.76) | copy-start | bytes 983044
  432.2 5.6 %copy-start.19 = (bf16[128,1280]{0,1:T(8,128)(2,1)S(1)}, bf16[128,1280]{0,1:T(8,128)(2,1)}, u32[]{:S(2)}) copy-start(bf16[128,1280]{0,1:T(8,128)(2,1)} %copy.77) | copy-start | bytes 983044
  432.2 5.7 %copy-start.20 = (bf16[128,1280]{0,1:T(8,128)(2,1)S(1)}, bf16[128,1280]{0,1:T(8,128)(2,1)}, u32[]{:S(2)}) copy-start(bf16[128,1280]{0,1:T(8,128)(2,1)} %copy.75) | copy-start | bytes 983044
  433.2 17.9 %collective-permute-start.8 = (bf16[128,8,160]{0,2,1:T(8,128)(2,1)}, bf16[128,8,160]{0,2,1:T(8,128)(2,1)}, u32[]{:S(2)}, u32[]{:S(2)}) collective-permute-start(bf16[128,8,160]{0,2,1:T(8,128)(2,1)} %get-tuple-element.20), channel_id=1, source_target_pairs={{0,63},{1,0},{2,1},{3,2},{4,3},{5,4},{6,5},{7,6},{8,7},{9,8},{10,9... | collective-permute-start | bytes 983048 | tf_op jit(solution)/shard_map/ppermute | solution.py:14
  435.3 16.4 %collective-permute-start.9 = (bf16[128,8,160]{0,2,1:T(8,128)(2,1)}, bf16[128,8,160]{0,2,1:T(8,128)(2,1)}, u32[]{:S(2)}, u32[]{:S(2)}) collective-permute-start(bf16[128,8,160]{0,2,1:T(8,128)(2,1)} %get-tuple-element.21), channel_id=1, source_target_pairs={{0,1},{1,2},{2,3},{3,4},{4,5},{5,6},{6,7},{7,8},{8,9},{9,10},{10,1... | collective-permute-start | bytes 983048 | tf_op jit(solution)/shard_map/ppermute | solution.py:14
  438.9 10.8 %copy-start.13 = (bf16[1,128,1280]{1,2,0:T(8,128)(2,1)S(1)}, bf16[1,128,1280]{1,2,0:T(8,128)(2,1)}, u32[]{:S(2)}) copy-start(bf16[1,128,1280]{1,2,0:T(8,128)(2,1)} %copy-done.12) | copy-start | bytes 983044
  438.9 10.8 %copy-start.16 = (bf16[128,1280]{0,1:T(8,128)(2,1)S(1)}, bf16[128,1280]{0,1:T(8,128)(2,1)}, u32[]{:S(2)}) copy-start(bf16[128,1280]{0,1:T(8,128)(2,1)} %copy-done.15) | copy-start | bytes 983044
  438.9 10.9 %copy-start.18 = (bf16[128,1280]{0,1:T(8,128)(2,1)S(1)}, bf16[128,1280]{0,1:T(8,128)(2,1)}, u32[]{:S(2)}) copy-start(bf16[128,1280]{0,1:T(8,128)(2,1)} %copy-done.17) | copy-start | bytes 983044
  440.2 13.9 %collective-permute-start.6 = (bf16[128,8,160]{0,2,1:T(8,128)(2,1)}, bf16[128,8,160]{0,2,1:T(8,128)(2,1)}, u32[]{:S(2)}, u32[]{:S(2)}) collective-permute-start(bf16[128,8,160]{0,2,1:T(8,128)(2,1)} %get-tuple-element.22), channel_id=1, source_target_pairs={{0,63},{1,0},{2,1},{3,2},{4,3},{5,4},{6,5},{7,6},{8,7},{9,8},{10,9... | collective-permute-start | bytes 983048 | tf_op jit(solution)/shard_map/ppermute | solution.py:14
  447.8 16.2 %collective-permute-start.7 = (bf16[128,8,160]{0,2,1:T(8,128)(2,1)S(1)}, bf16[128,8,160]{0,2,1:T(8,128)(2,1)}, u32[]{:S(2)}, u32[]{:S(2)}) collective-permute-start(bf16[128,8,160]{0,2,1:T(8,128)(2,1)S(1)} %get-tuple-element.23), channel_id=1, source_target_pairs={{0,1},{1,2},{2,3},{3,4},{4,5},{5,6},{6,7},{7,8},{8,9},{9,10},{10,1... | collective-permute-start | bytes 983048 | tf_op jit(solution)/shard_map/ppermute | solution.py:14
  (4 other events, 7.4 us)
Sparse Core Ops, SparseCore 0:
  10.7 81.2 all-gather.1
where the time goes:
time: 474 us; the launch traced here: 473 us
  blocking collectives  307 us (65%)
  starting transfers between devices  59.8 us (13%)
  waiting for transfers between devices  35.6 us (8%)
  local copies, waits for them, and re-layouts  26.6 us (6%)
  other arithmetic  18.1 us (4%)
  between operations  15.3 us (3%)
  matrix products  10.4 us (2%)
    psum x1, blocking collectives, local(): d_weight = lax.psum(weight_part, 'region').astype(jnp.bfloat16)  307 us
    ppermute x10, starting transfers between devices, from_behind(): lax.ppermute(value, axis, [(i, (i + by) % length) for i in range(length)])  43.7 us
    all_gather x1, waiting for transfers between devices, local(): gathered = lax.all_gather(grads, 'dp', axis=1, tiled=True)  20.1 us
    unnamed x62, local copies, waits for them, and re-layouts  16 us
    ppermute x10, waiting for transfers between devices, from_behind(): lax.ppermute(value, axis, [(i, (i + by) % length) for i in range(length)])  15.5 us
    unnamed x2, other arithmetic  12.4 us
    all_to_all x1, starting transfers between devices, local(): lax.all_to_all(attn_part.astype(jnp.bfloat16)[None], 'dp', split_axis=1,...  10.2 us
  transfers between devices with their start and end apart: 13, of which 4 were waited for; matrix products, arithmetic and copies ran while one was open for 5% of the time, Pallas kernels for 0%

commit v1 on v0

--- a/solution.py
+++ b/solution.py
@@ -47,7 +47,8 @@
     live_blocks = jnp.arange(BLK) < counts[0]
     live_rows = jnp.repeat(live_blocks, block_rows)
     grads = d_out * live_rows[None, :, None].astype(jnp.bfloat16)
-    gathered = lax.all_gather(grads, "dp", axis=1, tiled=True)
+    repeated = jnp.stack([grads] * lax.axis_size("dp"))
+    gathered = jnp.concatenate(lax.all_to_all(repeated, "dp", 0, 0), axis=1)
     out_cols = lax.all_to_all(attn_out, "dp", split_axis=2, concat_axis=1, tiled=True)
     attn_part = jnp.einsum("td,hd->th", gathered[0], w_out, preferred_element_type=jnp.float32)
     d_attn = lax.all_to_all(

time: 474 us -> 479 us (1.011)
  the two profiles are of different devices: /device:TPU:2 before, /device:TPU:4 now
where the time goes in v1:
time: 479 us; the launch traced here: 478 us
  blocking collectives  313 us (65%)
  starting transfers between devices  59 us (12%)
  waiting for transfers between devices  47.4 us (10%)
  local copies, waits for them, and re-layouts  26.9 us (6%)
  other arithmetic  15.8 us (3%)
  matrix products  13.9 us (3%)
    psum x1, blocking collectives, local(): d_weight = lax.psum(weight_part, 'region').astype(jnp.bfloat16)  313 us
    ppermute x10, waiting for transfers between devices, from_behind(): lax.ppermute(value, axis, [(i, (i + by) % length) for i in range(length)])  39.5 us
    ppermute x10, starting transfers between devices, from_behind(): lax.ppermute(value, axis, [(i, (i + by) % length) for i in range(length)])  37.8 us
    unnamed x50, local copies, waits for them, and re-layouts  16.1 us
    unnamed x2, other arithmetic  11.5 us
  transfers between devices with their start and end apart: 13, of which 4 were waited for; matrix products, arithmetic and copies ran while one was open for 5% of the time, Pallas kernels for 0%

profile of v1, /device:TPU:4, one launch (start us, length us, event | category | flops | bytes accessed | tf_op | source)
XLA Modules:
  0.0 478.0 jit_solution(2722282103875781250)
XLA Ops:
  0.7 1.5 copy.83
  2.7 7.4 %reduce.5 = bf16[1280,128]{1,0:T(8,128)(2,1)S(1)} reduce(bf16[1280,1,128]{2,1,0:T(2,128)(2,1)S(1)} %bitcast.100, bf16[]{:T(256)} %broadcast.43), dimensions={1}, to_apply=%bitcast.82.reduce_sub_computation | reduce | bytes 655362
  10.9 9.2 %all-to-all-start.2 = ((bf16[8,2,10240]{2,1,0:T(2,128)(2,1)}), bf16[8,2,10240]{2,1,0:T(2,128)(2,1)S(1)}, u32[]{:S(2)}, u32[]{:S(2)}) async-start(bf16[8,2,10240]{2,1,0:T(2,128)(2,1)} %reshape.84), calls=%async_computation.2 | async-start | bytes 655360 | tf_op jit(solution)/shard_map/all_to_all | solution.py:52
  21.1 4.0 all-to-all-done.2
  25.1 2.8 stack.2
  27.9 7.2 %all-to-all-start = ((bf16[8,1,128,2560]{3,2,1,0:T(8,128)(2,1)}), bf16[8,1,128,2560]{3,2,1,0:T(8,128)(2,1)}, u32[]{:S(2)}, u32[]{:S(2)}) async-start(bf16[8,1,128,2560]{3,2,1,0:T(8,128)(2,1)} %stack.2), calls=%async_computation | async-start | bytes 10485760 | tf_op jit(solution)/shard_map/all_to_all | solution.py:51
  35.1 2.0 collective-permute-start.2
  37.2 3.9 collective-permute-start
  41.1 6.1 %collective-permute-start.1 = (bf16[128,1280]{1,0:T(8,128)(2,1)S(1)}, bf16[128,1280]{1,0:T(8,128)(2,1)}, u32[]{:S(2)}, u32[]{:S(2)}) collective-permute-start(bf16[128,1280]{1,0:T(8,128)(2,1)S(1)} %bitcast.114), channel_id=1, source_target_pairs={{0,63},{1,0},{2,1},{3,2},{4,3},{5,4},{6,5},{7,6},{8,7},{9,8},{10,9... | collective-permute-start | bytes 983048 | tf_op jit(solution)/shard_map/ppermute | solution.py:14
  47.2 1.9 collective-permute-start.4
  49.2 7.9 %collective-permute-start.5 = (bf16[128,1280]{1,0:T(8,128)(2,1)S(1)}, bf16[128,1280]{1,0:T(8,128)(2,1)S(1)}, u32[]{:S(2)}, u32[]{:S(2)}) collective-permute-start(bf16[128,1280]{1,0:T(8,128)(2,1)S(1)} %bitcast.116), channel_id=1, source_target_pairs={{0,63},{1,0},{2,1},{3,2},{4,3},{5,4},{6,5},{7,6},{8,7},{9,8},{10,9... | collective-permute-start | bytes 983048 | tf_op jit(solution)/shard_map/ppermute | solution.py:14
  57.3 2.1 collective-permute-start.3
  61.5 30.5 %collective-permute-done.3 = bf16[128]{0:T(256)(128)(2,1)S(1)} collective-permute-done((bf16[128]{0:T(256)(128)(2,1)S(1)}, bf16[128]{0:T(256)(128)(2,1)S(1)}, u32[]{:S(2)}, u32[]{:S(2)}) %collective-permute-start.3) | collective-permute-done | bytes 288 | tf_op jit(solution)/shard_map/ppermute | solution.py:14
  93.8 1.3 copy.69
  99.6 3.9 all-to-all-done
  103.5 4.3 fusion.7
  108.7 4.0 reduce.4
  112.7 1.6 reshape.82
  114.3 4.8 %all-to-all-start.1 = ((bf16[8,2,10240]{2,1,0:T(2,128)(2,1)}), bf16[8,2,10240]{2,1,0:T(2,128)(2,1)S(1)}, u32[]{:S(2)}, u32[]{:S(2)}) async-start(bf16[8,2,10240]{2,1,0:T(2,128)(2,1)} %reshape.82), calls=%async_computation.1 | async-start | bytes 655360 | tf_op jit(solution)/shard_map/all_to_all | solution.py:54
  119.1 3.5 convolution_bitcast_fusion
  122.6 313.3 %all-reduce.1 = bf16[160,2560]{1,0:T(8,128)(2,1)} all-reduce(f32[160,2560]{1,0:T(8,128)S(1)} %convolution_bitcast_fusion), channel_id=1, replica_groups=mesh['dp'=8,'region'=64] {'region'}, use_global_device_ids=true, to_apply=%region_2.3 | all-reduce | flops 409600 | bytes 2457600 | tf_op jit(solution)/shard_map/psum | solution.py:60
  435.9 2.1 reshape.83
  438.0 1.3 copy.104
  439.5 1.8 fusion.34
  442.3 1.9 collective-permute-start.8
  444.2 2.6 collective-permute-start.9
  449.0 2.0 multiply_convert_fusion
  452.3 7.4 %collective-permute-start.6 = (bf16[128,8,160]{0,2,1:T(8,128)(2,1)}, bf16[128,8,160]{0,2,1:T(8,128)(2,1)}, u32[]{:S(2)}, u32[]{:S(2)}) collective-permute-start(bf16[128,8,160]{0,2,1:T(8,128)(2,1)} %get-tuple-element.22), channel_id=1, source_target_pairs={{0,63},{1,0},{2,1},{3,2},{4,3},{5,4},{6,5},{7,6},{8,7},{9,8},{10,9... | collective-permute-start | bytes 983048 | tf_op jit(solution)/shard_map/ppermute | solution.py:14
  459.7 1.9 collective-permute-start.7
  462.8 1.9 copy.85
  464.7 1.4 fusion.18
  467.0 9.0 %collective-permute-done.7 = bf16[128,8,160]{0,2,1:T(8,128)(2,1)} collective-permute-done((bf16[128,8,160]{0,2,1:T(8,128)(2,1)S(1)}, bf16[128,8,160]{0,2,1:T(8,128)(2,1)}, u32[]{:S(2)}, u32[]{:S(2)}) %collective-permute-start.7) | collective-permute-done | bytes 327712 | tf_op jit(solution)/shard_map/ppermute | solution.py:14
  (82 shorter events, 19.7 us)
Async XLA Ops:
  0.6 102.9 %copy-start = (bf16[160,2560]{1,0:T(8,128)(2,1)S(1)}, bf16[160,2560]{1,0:T(8,128)(2,1)}, u32[]{:S(2)}) copy-start(bf16[160,2560]{1,0:T(8,128)(2,1)} %param.13) | copy-start | bytes 2457604
  0.6 20.3 %copy-start.6 = (bf16[1,128,2560]{2,1,0:T(8,128)(2,1)S(1)}, bf16[1,128,2560]{2,1,0:T(8,128)(2,1)}, u32[]{:S(2)}) copy-start(bf16[1,128,2560]{2,1,0:T(8,128)(2,1)} %param.12) | copy-start | bytes 1966084
  10.9 14.2 %all-to-all-start.2 = ((bf16[8,2,10240]{2,1,0:T(2,128)(2,1)}), bf16[8,2,10240]{2,1,0:T(2,128)(2,1)S(1)}, u32[]{:S(2)}, u32[]{:S(2)}) async-start(bf16[8,2,10240]{2,1,0:T(2,128)(2,1)} %reshape.84), calls=%async_computation.2 | async-start | bytes 655360 | tf_op jit(solution)/shard_map/all_to_all | solution.py:52
  27.9 9.3 %copy-start.8 = (bf16[1,128,1280]{2,1,0:T(8,128)(2,1)S(1)}, bf16[1,128,1280]{2,1,0:T(8,128)(2,1)}, u32[]{:S(2)}) copy-start(bf16[1,128,1280]{2,1,0:T(8,128)(2,1)} %param.9) | copy-start | bytes 983044
  27.9 19.3 %copy-start.9 = (bf16[1,128,1280]{2,1,0:T(8,128)(2,1)S(1)}, bf16[1,128,1280]{2,1,0:T(8,128)(2,1)}, u32[]{:S(2)}) copy-start(bf16[1,128,1280]{2,1,0:T(8,128)(2,1)} %param.10) | copy-start | bytes 983044
  27.9 31.5 %copy-start.3 = (bf16[1,128,1280]{2,1,0:T(8,128)(2,1)S(1)}, bf16[1,128,1280]{2,1,0:T(8,128)(2,1)}, u32[]{:S(2)}) copy-start(bf16[1,128,1280]{2,1,0:T(8,128)(2,1)} %param.11) | copy-start | bytes 983044
  27.9 75.6 %all-to-all-start = ((bf16[8,1,128,2560]{3,2,1,0:T(8,128)(2,1)}), bf16[8,1,128,2560]{3,2,1,0:T(8,128)(2,1)}, u32[]{:S(2)}, u32[]{:S(2)}) async-start(bf16[8,1,128,2560]{3,2,1,0:T(8,128)(2,1)} %stack.2), calls=%async_computation | async-start | bytes 10485760 | tf_op jit(solution)/shard_map/all_to_all | solution.py:51
  35.1 26.1 %copy-start.7 = (bf16[1,128,1280]{2,1,0:T(8,128)(2,1)S(1)}, bf16[1,128,1280]{2,1,0:T(8,128)(2,1)}, u32[]{:S(2)}) copy-start(bf16[1,128,1280]{2,1,0:T(8,128)(2,1)} %param.8) | copy-start | bytes 983044
  35.1 57.1 %copy-start.16 = (s32[1,4,12]{2,1,0:T(4,128)S(1)}, s32[1,4,12]{2,1,0:T(4,128)}, u32[]{:S(2)}) copy-start(s32[1,4,12]{2,1,0:T(4,128)} %param.14) | copy-start | bytes 580
  35.1 22.1 %collective-permute-start.2 = (bf16[128]{0:T(256)(128)(2,1)S(1)}, bf16[128]{0:T(256)(128)(2,1)S(1)}, u32[]{:S(2)}, u32[]{:S(2)}) collective-permute-start(bf16[128]{0:T(256)(128)(2,1)S(1)} %convert_element_type.56), channel_id=1, source_target_pairs={{0,1},{1,2},{2,3},{3,4},{4,5},{5,6},{6,7},{7,8},{8,9},{9,10},{10,1... | collective-permute-start | bytes 776 | tf_op jit(solution)/shard_map/ppermute | solution.py:14
  37.2 55.4 %collective-permute-start = (bf16[128,1280]{1,0:T(8,128)(2,1)S(1)}, bf16[128,1280]{1,0:T(8,128)(2,1)}, u32[]{:S(2)}, u32[]{:S(2)}) collective-permute-start(bf16[128,1280]{1,0:T(8,128)(2,1)S(1)} %bitcast.113), channel_id=1, source_target_pairs={{0,1},{1,2},{2,3},{3,4},{4,5},{5,6},{6,7},{7,8},{8,9},{9,10},{10,1... | collective-permute-start | bytes 983048 | tf_op jit(solution)/shard_map/ppermute | solution.py:14
  41.1 52.7 %collective-permute-start.1 = (bf16[128,1280]{1,0:T(8,128)(2,1)S(1)}, bf16[128,1280]{1,0:T(8,128)(2,1)}, u32[]{:S(2)}, u32[]{:S(2)}) collective-permute-start(bf16[128,1280]{1,0:T(8,128)(2,1)S(1)} %bitcast.114), channel_id=1, source_target_pairs={{0,63},{1,0},{2,1},{3,2},{4,3},{5,4},{6,5},{7,6},{8,7},{9,8},{10,9... | collective-permute-start | bytes 983048 | tf_op jit(solution)/shard_map/ppermute | solution.py:14
  47.2 47.9 %collective-permute-start.4 = (bf16[128,1280]{1,0:T(8,128)(2,1)S(1)}, bf16[128,1280]{1,0:T(8,128)(2,1)S(1)}, u32[]{:S(2)}, u32[]{:S(2)}) collective-permute-start(bf16[128,1280]{1,0:T(8,128)(2,1)S(1)} %bitcast.115), channel_id=1, source_target_pairs={{0,1},{1,2},{2,3},{3,4},{4,5},{5,6},{6,7},{7,8},{8,9},{9,10},{10,1... | collective-permute-start | bytes 983048 | tf_op jit(solution)/shard_map/ppermute | solution.py:14
  49.2 46.8 %collective-permute-start.5 = (bf16[128,1280]{1,0:T(8,128)(2,1)S(1)}, bf16[128,1280]{1,0:T(8,128)(2,1)S(1)}, u32[]{:S(2)}, u32[]{:S(2)}) collective-permute-start(bf16[128,1280]{1,0:T(8,128)(2,1)S(1)} %bitcast.116), channel_id=1, source_target_pairs={{0,63},{1,0},{2,1},{3,2},{4,3},{5,4},{6,5},{7,6},{8,7},{9,8},{10,9... | collective-permute-start | bytes 983048 | tf_op jit(solution)/shard_map/ppermute | solution.py:14
  57.2 39.7 %copy-start.10 = (bf16[1,128,1280]{1,2,0:T(8,128)(2,1)}, bf16[1,128,1280]{1,2,0:T(8,128)(2,1)S(1)}, u32[]{:S(2)}) copy-start(bf16[1,128,1280]{1,2,0:T(8,128)(2,1)S(1)} %copy.68) | copy-start | bytes 983044
  57.3 34.7 %collective-permute-start.3 = (bf16[128]{0:T(256)(128)(2,1)S(1)}, bf16[128]{0:T(256)(128)(2,1)S(1)}, u32[]{:S(2)}, u32[]{:S(2)}) collective-permute-start(bf16[128]{0:T(256)(128)(2,1)S(1)} %convert_element_type.56), channel_id=1, source_target_pairs={{0,63},{1,0},{2,1},{3,2},{4,3},{5,4},{6,5},{7,6},{8,7},{9,8},{10,9... | collective-permute-start | bytes 776 | tf_op jit(solution)/shard_map/ppermute | solution.py:14
  61.4 36.2 %copy-start.4 = (bf16[1,128,1280]{1,2,0:T(8,128)(2,1)}, bf16[1,128,1280]{1,2,0:T(8,128)(2,1)S(1)}, u32[]{:S(2)}) copy-start(bf16[1,128,1280]{1,2,0:T(8,128)(2,1)S(1)} %copy.71) | copy-start | bytes 983044
  93.8 3.9 copy-start.12
  95.1 2.6 copy-start.14
  97.6 1.1 copy-start.1
  114.3 321.6 %all-to-all-start.1 = ((bf16[8,2,10240]{2,1,0:T(2,128)(2,1)}), bf16[8,2,10240]{2,1,0:T(2,128)(2,1)S(1)}, u32[]{:S(2)}, u32[]{:S(2)}) async-start(bf16[8,2,10240]{2,1,0:T(2,128)(2,1)} %reshape.82), calls=%async_computation.1 | async-start | bytes 655360 | tf_op jit(solution)/shard_map/all_to_all | solution.py:54
  435.9 3.6 copy-start.2
  442.3 22.4 %collective-permute-start.8 = (bf16[128,8,160]{0,2,1:T(8,128)(2,1)}, bf16[128,8,160]{0,2,1:T(8,128)(2,1)}, u32[]{:S(2)}, u32[]{:S(2)}) collective-permute-start(bf16[128,8,160]{0,2,1:T(8,128)(2,1)} %get-tuple-element.20), channel_id=1, source_target_pairs={{0,63},{1,0},{2,1},{3,2},{4,3},{5,4},{6,5},{7,6},{8,7},{9,8},{10,9... | collective-permute-start | bytes 983048 | tf_op jit(solution)/shard_map/ppermute | solution.py:14
  444.2 20.5 %collective-permute-start.9 = (bf16[128,8,160]{0,2,1:T(8,128)(2,1)}, bf16[128,8,160]{0,2,1:T(8,128)(2,1)}, u32[]{:S(2)}, u32[]{:S(2)}) collective-permute-start(bf16[128,8,160]{0,2,1:T(8,128)(2,1)} %get-tuple-element.21), channel_id=1, source_target_pairs={{0,1},{1,2},{2,3},{3,4},{4,5},{5,6},{6,7},{7,8},{8,9},{9,10},{10,1... | collective-permute-start | bytes 983048 | tf_op jit(solution)/shard_map/ppermute | solution.py:14
  448.9 2.0 copy-start.5
  451.0 10.6 %copy-start.11 = (bf16[1,128,1280]{1,2,0:T(8,128)(2,1)S(1)}, bf16[1,128,1280]{1,2,0:T(8,128)(2,1)}, u32[]{:S(2)}) copy-start(bf16[1,128,1280]{1,2,0:T(8,128)(2,1)} %copy-done.10) | copy-start | bytes 983044
  451.0 10.6 %copy-start.13 = (bf16[128,1280]{0,1:T(8,128)(2,1)S(1)}, bf16[128,1280]{0,1:T(8,128)(2,1)}, u32[]{:S(2)}) copy-start(bf16[128,1280]{0,1:T(8,128)(2,1)} %copy-done.12) | copy-start | bytes 983044
  451.0 10.6 %copy-start.15 = (bf16[128,1280]{0,1:T(8,128)(2,1)S(1)}, bf16[128,1280]{0,1:T(8,128)(2,1)}, u32[]{:S(2)}) copy-start(bf16[128,1280]{0,1:T(8,128)(2,1)} %copy-done.14) | copy-start | bytes 983044
  452.3 14.7 %collective-permute-start.6 = (bf16[128,8,160]{0,2,1:T(8,128)(2,1)}, bf16[128,8,160]{0,2,1:T(8,128)(2,1)}, u32[]{:S(2)}, u32[]{:S(2)}) collective-permute-start(bf16[128,8,160]{0,2,1:T(8,128)(2,1)} %get-tuple-element.22), channel_id=1, source_target_pairs={{0,63},{1,0},{2,1},{3,2},{4,3},{5,4},{6,5},{7,6},{8,7},{9,8},{10,9... | collective-permute-start | bytes 983048 | tf_op jit(solution)/shard_map/ppermute | solution.py:14
  459.7 16.2 %collective-permute-start.7 = (bf16[128,8,160]{0,2,1:T(8,128)(2,1)S(1)}, bf16[128,8,160]{0,2,1:T(8,128)(2,1)}, u32[]{:S(2)}, u32[]{:S(2)}) collective-permute-start(bf16[128,8,160]{0,2,1:T(8,128)(2,1)S(1)} %get-tuple-element.23), channel_id=1, source_target_pairs={{0,1},{1,2},{2,3},{3,4},{4,5},{5,6},{6,7},{7,8},{8,9},{9,10},{10,1... | collective-permute-start | bytes 983048 | tf_op jit(solution)/shard_map/ppermute | solution.py:14
